TPU v7x, 32 devices: a whole 2x2x4 slice. The times are simulated.
32 devices in a mesh: task: 16 (over z, x, core), tensor: 2 (over y).
Axes of the slice: x: 2, y: 2, z: 4, core: 2. Of those that a mesh axis runs over, the one named last changes fastest.
Arguments:
- inputs: bfloat16 [3072, 8192], P('task'), may hold values from -6 to 6
- queries: bfloat16 [3072, 4096], P('task', 'tensor'), may hold values from -6 to 6
- task_vectors: bfloat16 [8, 2, 8192, 1024], P(None, None, 'task', 'tensor'), may hold values from -0.0625 to 0.0625
- base_weights: bfloat16 [2, 8192, 1024], P(None, 'task', 'tensor'), may hold values from -0.0625 to 0.0625
- scale_exps: int32 [8, 2, 64, 8], P(None, None, 'task', 'tensor'), may hold values from -3 to 0
- coefs: float32 [8, 2], replicated, may hold values from 0.1 to 0.6
Outputs:
- attended: bfloat16 [3072, 4096], P('task', 'tensor')
- mean_entropy: float32 [], replicated
- coef_grad: float32 [8, 2], replicated
All inputs are finite; a program needn't handle non-finite values.
Results may differ from a plain program's by a relative error of at most 0.0087.
Values may be sent and summed in bfloat16 or wider, within the bound.
A program may use at most 128 MiB of HBM per device.

v0:
```python
import jax
import jax.numpy as jnp
from jax import lax
from jax.sharding import PartitionSpec as P

HEAD = 128
GROUP = 4
sharpen = 4.0
capping = 8.0
masked_value = -1e30


def dequantize(vectors, exponents):
    tasks, mats, rows, cols = vectors.shape
    row_blocks = exponents.shape[2]
    col_blocks = exponents.shape[3]
    factor = jnp.exp2(exponents.astype(jnp.float32))
    blocked = vectors.astype(jnp.float32).reshape(
        tasks, mats, row_blocks, rows // row_blocks, col_blocks, cols // col_blocks
    )
    blocked = blocked * factor[:, :, :, None, :, None]
    return blocked.reshape(tasks, mats, rows, cols)


def capped_logits(attended):
    return capping * jnp.tanh(sharpen * attended.astype(jnp.float32) / capping)


def entropy_grad(logits, expo, total, moment):
    average = moment / total
    entropy = jnp.log(total) - average
    slope = sharpen * (1.0 - (logits / capping) ** 2)
    d_out = (slope * (-(expo / total[:, None]) * (logits - average[:, None]))).astype(jnp.bfloat16)
    return (entropy, d_out)


def local(inputs, queries, task_vectors, base_weights, scale_exps, coefs):
    n_task = lax.axis_size("task")
    n_tensor = lax.axis_size("tensor")
    tok_count = inputs.shape[0]
    col_dev = task_vectors.shape[3]
    kv_local = col_dev // HEAD
    scaled = dequantize(task_vectors, scale_exps)
    merged = (
        base_weights.astype(jnp.float32) + jnp.sum(coefs[:, :, None, None] * scaled, axis=0)
    ).astype(jnp.bfloat16)
    projected = jnp.einsum(
        "td,mdc->mtc",
        inputs,
        lax.all_gather(merged, "task", axis=1, tiled=True),
        preferred_element_type=jnp.float32,
    )
    projected_b = projected.astype(jnp.bfloat16)
    keys_b = projected_b[0].reshape(tok_count, kv_local, HEAD)
    values_b = projected_b[1].reshape(tok_count, kv_local, HEAD)
    query_heads = queries.reshape(tok_count, kv_local, GROUP, HEAD)
    inverse = HEAD ** (-0.5)
    scores = (
        jnp.einsum("shrd,thd->hrst", query_heads, keys_b, preferred_element_type=jnp.float32)
        * inverse
    )
    position = jnp.arange(tok_count)
    causal = position[None, :] <= position[:, None]
    scores = jnp.where(causal, scores, masked_value)
    probs = jax.nn.softmax(scores, axis=-1)
    probs_b = probs.astype(jnp.bfloat16)
    outputs = jnp.einsum("hrst,thd->shrd", probs_b, values_b, preferred_element_type=jnp.float32)
    attended = outputs.astype(jnp.bfloat16).reshape(tok_count, kv_local * GROUP * HEAD)
    logits = capped_logits(attended)
    expo = jnp.exp(logits)
    total, moment = lax.psum((jnp.sum(expo, axis=1), jnp.sum(expo * logits, axis=1)), "tensor")
    entropy, d_out = entropy_grad(logits, expo, total, moment)
    entropy_part = jnp.sum(entropy) / n_tensor
    d_out_heads = d_out.reshape(tok_count, kv_local, GROUP, HEAD)
    d_probs = jnp.einsum(
        "shrd,thd->hrst", d_out_heads, values_b, preferred_element_type=jnp.float32
    )
    d_scores = (probs * (d_probs - jnp.sum(probs * d_probs, axis=-1, keepdims=True))).astype(
        jnp.bfloat16
    )
    d_keys = (
        jnp.einsum("hrst,shrd->thd", d_scores, query_heads, preferred_element_type=jnp.float32)
        * inverse
    )
    d_values = jnp.einsum(
        "hrst,shrd->thd", probs_b, d_out_heads, preferred_element_type=jnp.float32
    )
    d_kv = jnp.stack(
        [d_keys.reshape(tok_count, col_dev), d_values.reshape(tok_count, col_dev)]
    ).astype(jnp.bfloat16)
    input_rows = lax.all_to_all(inputs, "task", split_axis=1, concat_axis=0, tiled=True)
    weight_grads = jnp.einsum(
        "tr,mtc->mrc",
        input_rows,
        lax.all_gather(d_kv, "task", axis=1, tiled=True),
        preferred_element_type=jnp.float32,
    )
    coef_part = jnp.sum(weight_grads[None] * scaled, axis=(2, 3))
    entropy_sum, coef_grad = lax.psum((entropy_part, coef_part), ("task", "tensor"))
    mean_entropy = entropy_sum / (tok_count * n_task)
    return (attended, mean_entropy, coef_grad)


def solution(mesh):
    return jax.shard_map(
        local,
        mesh=mesh,
        in_specs=(
            P("task", None),
            P("task", "tensor"),
            P(None, None, "task", "tensor"),
            P(None, "task", "tensor"),
            P(None, None, "task", "tensor"),
            P(),
        ),
        out_specs=(P("task", "tensor"), P(), P()),
        check_vma=False,
    )
```

profile of v0, /device:TPU:0, one launch (start us, length us, event | category | flops | bytes accessed | tf_op | source)
XLA Modules:
  0.0 388.9 jit_solution(6853657786691911180)
XLA Ops:
  7.2 0.7 multiply_exponential_fusion
  8.1 6.1 %mul.78 = f32[8,2,4,128,4,128]{5,4,3,2,1,0:T(4,128)} broadcast(f32[8,2,4,4]{3,2,1,0:T(4,128)S(1)} %copy.33), dimensions={0,1,2,4} | broadcast | bytes 16778240 | tf_op jit(solution)/shard_map/mul | solution.py:21
  14.2 19.9 %mul.79 = f32[8,2,512,512]{3,2,1,0:T(8,128)} reshape(f32[8,2,4,128,4,128]{5,4,3,2,1,0:T(4,128)} %mul.78) | data formatting | bytes 33554432 | tf_op jit(solution)/shard_map/mul | solution.py:21
  34.2 9.7 %multiply_reduce_fusion.1 = f32[2,512,512]{2,1,0:T(8,128)S(1)} fusion(f32[8,2,512,512]{3,2,1,0:T(8,128)} %mul.79, bf16[8,2,512,512]{3,2,1,0:T(8,128)(2,1)} %param.8, f32[8,2]{1,0:T(8,128)S(1)} %copy.32), kind=kLoop, calls=%fused_computation.2 | loop fusion | flops 16252928 | bytes 27263040 | tf_op jit(solution)/shard_map/reduce_sum | solution.py:45
  43.9 1.4 add_convert_fusion
  45.3 3.0 reshape.37
  48.9 125.7 %all-gather.3.cloned.1.call-done = bf16[2,8192,512]{2,1,0:T(8,128)(2,1)} async-done(((bf16[2,512,512]{2,1,0:T(8,128)(2,1)}), bf16[2,8192,512]{2,1,0:T(8,128)(2,1)}) %all-gather.3.cloned.1.call-update) | async-done | bytes 16777232 | tf_op jit(solution)/shard_map/all_gather | solution.py:50
  174.6 7.6 %fusion.26 = bf16[2,192,512]{2,1,0:T(8,128)(2,1)S(1)} fusion(bf16[2,8192,512]{2,1,0:T(8,128)(2,1)} %all-gather.3.cloned.1.call-done, bf16[192,8192]{1,0:T(8,128)(2,1)S(1)} %copy-done), kind=kOutput, calls=%fused_computation.38 | convolution fusion | flops 3221422080 | bytes 20316160 | tf_op jit(solution)/shard_map/td,mdc->mtc/dot_general | solution.py:47
  182.2 0.7 fusion.53
  182.9 1.0 reshape_squeeze.7
  183.9 0.7 reshape_squeeze.6
  184.6 1.7 fusion.43
  186.4 1.0 fusion.54
  187.4 1.9 exponential_reduce_fusion
  189.4 4.9 %all-reduce.1 = (f32[192]{0:T(256)S(1)}, f32[192]{0:T(256)S(1)}) all-reduce(f32[192]{0:T(256)S(1)} %get-tuple-element.7, f32[192]{0:T(256)S(1)} %get-tuple-element.6), channel_id=1, replica_groups=mesh['task'=16,'tensor'=2] {'tensor'}, use_global_device_ids=true, to_apply=%region_6.7 | all-reduce | flops 384 | bytes 3072 | tf_op jit(solution)/shard_map/psum | solution.py:71
  194.9 3.6 fusion.1
  198.5 1.9 fusion.36
  200.5 0.9 fusion.37
  201.6 1.1 copy.42
  202.7 0.8 stack_reshape.9
  203.4 1.7 pad_maximum_fusion
  205.1 2.0 copy.74
  207.2 3.9 %all-to-all-start = ((bf16[192,16,512]{2,0,1:T(8,128)(2,1)}), bf16[192,16,512]{2,0,1:T(8,128)(2,1)S(1)}, u32[]{:S(2)}, u32[]{:S(2)}) async-start(bf16[192,16,512]{2,0,1:T(8,128)(2,1)} %bitcast.76), calls=%async_computation | async-start | bytes 6291456 | tf_op jit(solution)/shard_map/all_to_all | solution.py:91
  211.1 2.6 copy.38
  214.4 92.6 %all-to-all-done = bf16[192,16,512]{2,0,1:T(8,128)(2,1)S(1)} async-done(((bf16[192,16,512]{2,0,1:T(8,128)(2,1)}), bf16[192,16,512]{2,0,1:T(8,128)(2,1)S(1)}, u32[]{:S(2)}, u32[]{:S(2)}) %all-to-all-start) | async-done | bytes 3145760 | tf_op jit(solution)/shard_map/all_to_all | solution.py:91
  307.0 4.0 %all-gather.5.cloned.1.call-done = bf16[2,3072,512]{2,1,0:T(8,128)(2,1)} async-done(((bf16[2,192,512]{2,1,0:T(8,128)(2,1)}), bf16[2,3072,512]{2,1,0:T(8,128)(2,1)}) %all-gather.5.cloned.1.call-update) | async-done | bytes 6291472 | tf_op jit(solution)/shard_map/all_gather | solution.py:95
  311.0 7.6 %convolution_bitcast_fusion = f32[2,512,512]{1,2,0:T(8,128)} fusion(bf16[2,3072,512]{2,1,0:T(8,128)(2,1)} %all-gather.5.cloned.1.call-done, bf16[3072,512,1]{1,0,2:T(8,128)(2,1)S(1)} %bitcast.78), kind=kOutput, calls=%fused_computation.19 | convolution fusion | flops 3221225472 | bytes 11534336 | tf_op jit(solution)/shard_map/tr,mtc->mrc/dot_general | solution.py:92
  318.5 1.9 copy.44
  320.5 9.3 %multiply_reduce_fusion = f32[8,2]{1,0:T(8,128)S(1)} fusion(f32[8,2,512,512]{3,2,1,0:T(8,128)} %mul.79, bf16[8,2,512,512]{3,2,1,0:T(8,128)(2,1)} %param.8, f32[2,512,512]{2,1,0:T(8,128)S(1)} %copy.44), kind=kLoop, calls=%fused_computation.1 | loop fusion | flops 16777200 | bytes 27263040 | tf_op jit(solution)/shard_map/reduce_sum | solution.py:98
  329.8 1.5 reshape.38
  331.3 48.3 %all-reduce = (f32[]{:T(128)}, f32[8,2]{1,0:T(8,128)S(1)}) all-reduce(f32[]{:T(128)S(6)} %div.37, f32[8,2]{1,0:T(8,128)S(1)} %multiply_reduce_fusion), channel_id=1, replica_groups=mesh['task'=16,'tensor'=2] {'task','tensor'}, use_global_device_ids=true, to_apply=%region_8.9 | all-reduce | flops 17 | bytes 136 | tf_op jit(solution)/shard_map/psum | solution.py:99
  379.6 0.6 copy.45
  (30 shorter events, 1.8 us)
Async XLA Ops:
  7.2 167.4 %all-gather.3.cloned.1.call-start = ((), (), s32[]{:S(2)}) async-start(), calls=%async_computation.1 | async-start | bytes 17825792 | tf_op jit(solution)/shard_map/all_gather | solution.py:50
  14.2 19.9 %copy-start.7 = (f32[8,2]{0,1:T(2,128)S(1)}, f32[8,2]{0,1:T(2,128)}, u32[]{:S(2)}) copy-start(f32[8,2]{0,1:T(2,128)} %param.11) | copy-start | bytes 196
  34.2 9.7 %copy-start.3 = (bf16[2,512,512]{2,1,0:T(8,128)(2,1)S(1)}, bf16[2,512,512]{2,1,0:T(8,128)(2,1)}, u32[]{:S(2)}) copy-start(bf16[2,512,512]{2,1,0:T(8,128)(2,1)} %param.9) | copy-start | bytes 3145732
  43.9 130.7 %copy-start = (bf16[192,8192]{1,0:T(8,128)(2,1)S(1)}, bf16[192,8192]{1,0:T(8,128)(2,1)}, u32[]{:S(2)}) copy-start(bf16[192,8192]{1,0:T(8,128)(2,1)} %param.6) | copy-start | bytes 9437188
  45.3 265.7 %all-gather.5.cloned.1.call-start = ((), (), s32[]{:S(2)}) async-start(), calls=%async_computation.2 | async-start | bytes 6684672 | tf_op jit(solution)/shard_map/all_gather | solution.py:95
  184.6 1.8 copy-start.6
  186.4 1.1 copy-start.5
  187.4 1.9 copy-start.8
  194.9 3.6 copy-start.4
  194.9 3.6 copy-start.9
  198.5 1.9 copy-start.2
  207.2 99.8 %all-to-all-start = ((bf16[192,16,512]{2,0,1:T(8,128)(2,1)}), bf16[192,16,512]{2,0,1:T(8,128)(2,1)S(1)}, u32[]{:S(2)}, u32[]{:S(2)}) async-start(bf16[192,16,512]{2,0,1:T(8,128)(2,1)} %bitcast.76), calls=%async_computation | async-start | bytes 6291456 | tf_op jit(solution)/shard_map/all_to_all | solution.py:91
  320.5 9.3 %copy-start.1 = (bf16[192,4,4,128]{3,2,1,0:T(4,128)(2,1)S(1)}, bf16[192,4,4,128]{3,2,1,0:T(4,128)(2,1)}, u32[]{:S(2)}) copy-start(bf16[192,4,4,128]{3,2,1,0:T(4,128)(2,1)} %copy.38) | copy-start | bytes 2359300
Sparse Core Ops, SparseCore 0:
  45.4 129.1 all-gather.2
  205.3 105.6 all-gather.4
where the time goes:
time: 390 us; the launch traced here: 389 us
  waiting for transfers between devices  222 us (57%)
  blocking collectives  53.2 us (14%)
  local copies, waits for them, and re-layouts  42.4 us (11%)
  matrix products  25.2 us (6%)
  other arithmetic  25.1 us (6%)
  between operations  16.6 us (4%)
  starting transfers between devices  4 us (1%)
    all_gather x1, waiting for transfers between devices, local(): lax.all_gather(merged, 'task', axis=1, tiled=True)  126 us
    all_to_all x1, waiting for transfers between devices, local(): lax.all_to_all(inputs, 'task', split_axis=1, concat_axis=0, tiled=True)  92.6 us
    psum x1, blocking collectives, local(): lax.psum((entropy_part, coef_part), ('task', 'tensor'))  48.3 us
    mul x2, local copies, waits for them, and re-layouts, dequantize(): blocked = blocked * factor[:, :, :, None, :, None]  26 us
    reduce_sum x1, other arithmetic, local(): jnp.sum(coefs[:, :, None, None] * scaled, axis=0)  9.68 us
    reduce_sum x1, other arithmetic, local(): coef_part = jnp.sum(weight_grads[None] * scaled, axis=(2, 3))  9.33 us
  transfers between devices with their start and end apart: 3, of which 3 were waited for; matrix products, arithmetic and copies ran while one was open for 2% of the time, Pallas kernels for 0%

commit v1 on v0

--- a/solution.py
+++ b/solution.py
@@ -44,12 +44,38 @@
     merged = (
         base_weights.astype(jnp.float32) + jnp.sum(coefs[:, :, None, None] * scaled, axis=0)
     ).astype(jnp.bfloat16)
-    projected = jnp.einsum(
+    size, index, width = (lax.axis_size("task"), lax.axis_index("task"), merged.shape[1])
+    right = [(i, (i + 1) % size) for i in range(size)]
+    left = [(i, (i - 1) % size) for i in range(size)]
+    middle = size // 2
+    from_left = from_right = merged
+    total_2 = jnp.einsum(
         "td,mdc->mtc",
-        inputs,
-        lax.all_gather(merged, "task", axis=1, tiled=True),
+        lax.dynamic_slice_in_dim(inputs, index * width, merged.shape[1], axis=1),
+        merged,
         preferred_element_type=jnp.float32,
     )
+    for step in range(1, middle + 1):
+        from_left = lax.ppermute(from_left, "task", right)
+        if step < size - middle:
+            from_right = lax.ppermute(from_right, "task", left)
+            total_2 = total_2 + jnp.einsum(
+                "td,mdc->mtc",
+                lax.dynamic_slice_in_dim(
+                    inputs, (index + step) % size * width, from_right.shape[1], axis=1
+                ),
+                from_right,
+                preferred_element_type=jnp.float32,
+            )
+        total_2 = total_2 + jnp.einsum(
+            "td,mdc->mtc",
+            lax.dynamic_slice_in_dim(
+                inputs, (index - step) % size * width, from_left.shape[1], axis=1
+            ),
+            from_left,
+            preferred_element_type=jnp.float32,
+        )
+    projected = total_2
     projected_b = projected.astype(jnp.bfloat16)
     keys_b = projected_b[0].reshape(tok_count, kv_local, HEAD)
     values_b = projected_b[1].reshape(tok_count, kv_local, HEAD)

time: 390 us -> 447 us (1.15)
  starting transfers between devices: 4 us -> 152 us
  waiting for transfers between devices: 222 us -> 123 us
  matrix products: 25.2 us -> 31.2 us
    ppermute x0 -> x15, starting transfers between devices: none -> 134 us  [the longest x8 128 us: local(): from_left = lax.ppermute(from_left, 'task', right)]
    all_gather x1 -> x0, waiting for transfers between devices: 126 us -> none  [local(): lax.all_gather(merged, 'task', axis=1, tiled=True)]
    ppermute x0 -> x15, waiting for transfers between devices: none -> 27.3 us  [the longest x8 27.3 us: local(): from_left = lax.ppermute(from_left, 'task', right)]
    all_to_all x1, starting transfers between devices: 3.92 us -> 18.5 us  [local(): lax.all_to_all(inputs, 'task', split_axis=1, concat_axis=0, tiled=True)]
    dot_general x1 -> x16, matrix products: 7.62 us -> 13.6 us  [the longest x7 6.49 us: local(): jnp.einsum('td,mdc->mtc', lax.dynamic_slice_in_dim(inputs, (index + step)...]
  transfers between devices with their start and end apart: 3 -> 17, of which waited for: 3 -> 7; matrix products, arithmetic and copies ran while one was open for 2% -> 5% of each run, Pallas kernels for 0% -> 0%
where the time goes in v1:
time: 447 us; the launch traced here: 446 us
  starting transfers between devices  152 us (34%)
  waiting for transfers between devices  123 us (28%)
  blocking collectives  54.3 us (12%)
  local copies, waits for them, and re-layouts  44 us (10%)
  matrix products  31.2 us (7%)
  other arithmetic  24.1 us (5%)
  between operations  16.9 us (4%)
    ppermute x8, starting transfers between devices, local(): from_left = lax.ppermute(from_left, 'task', right)  128 us
    all_to_all x1, waiting for transfers between devices, local(): lax.all_to_all(inputs, 'task', split_axis=1, concat_axis=0, tiled=True)  92.3 us
    psum x1, blocking collectives, local(): lax.psum((entropy_part, coef_part), ('task', 'tensor'))  49.4 us
    ppermute x8, waiting for transfers between devices, local(): from_left = lax.ppermute(from_left, 'task', right)  27.3 us
    mul x2, local copies, waits for them, and re-layouts, dequantize(): blocked = blocked * factor[:, :, :, None, :, None]  26 us
    all_to_all x1, starting transfers between devices, local(): lax.all_to_all(inputs, 'task', split_axis=1, concat_axis=0, tiled=True)  18.5 us
    reduce_sum x1, other arithmetic, local(): jnp.sum(coefs[:, :, None, None] * scaled, axis=0)  9.68 us
    reduce_sum x1, other arithmetic, local(): coef_part = jnp.sum(weight_grads[None] * scaled, axis=(2, 3))  9.33 us
  transfers between devices with their start and end apart: 17, of which 7 were waited for; matrix products, arithmetic and copies ran while one was open for 5% of the time, Pallas kernels for 0%

profile of v1, /device:TPU:0, one launch (start us, length us, event | category | flops | bytes accessed | tf_op | source)
XLA Modules:
  0.0 445.6 jit_solution(12020276156993527507)
XLA Ops:
  8.1 6.1 %mul.126 = f32[8,2,4,128,4,128]{5,4,3,2,1,0:T(4,128)} broadcast(f32[8,2,4,4]{3,2,1,0:T(4,128)S(1)} %copy.33), dimensions={0,1,2,4} | broadcast | bytes 16778240 | tf_op jit(solution)/shard_map/mul | solution.py:21
  14.2 19.9 %mul.127 = f32[8,2,512,512]{3,2,1,0:T(8,128)} reshape(f32[8,2,4,128,4,128]{5,4,3,2,1,0:T(4,128)} %mul.126) | data formatting | bytes 33554432 | tf_op jit(solution)/shard_map/mul | solution.py:21
  34.2 9.7 %multiply_reduce_fusion.1 = f32[2,512,512]{2,1,0:T(8,128)S(1)} fusion(f32[8,2,512,512]{3,2,1,0:T(8,128)} %mul.127, bf16[8,2,512,512]{3,2,1,0:T(8,128)(2,1)} %param.8, f32[8,2]{1,0:T(8,128)S(1)} %copy.32), kind=kLoop, calls=%fused_computation.2 | loop fusion | flops 16252928 | bytes 27263040 | tf_op jit(solution)/shard_map/reduce_sum | solution.py:45
  45.3 5.4 %collective-permute-start = (bf16[2,512,512]{2,1,0:T(8,128)(2,1)S(1)}, bf16[2,512,512]{2,1,0:T(8,128)(2,1)S(1)}, u32[]{:S(2)}, u32[]{:S(2)}) collective-permute-start(bf16[2,512,512]{2,1,0:T(8,128)(2,1)S(1)} %add_convert_fusion), channel_id=1, source_target_pairs={{0,30},{2,0},{4,2},{6,4},{8,6},{10,8},{12,10},{14,12},{16,14},{18,... | collective-permute-start | bytes 3145736 | tf_op jit(solution)/shard_map/ppermute | solution.py:61
  50.7 11.6 %collective-permute-done.1 = bf16[2,512,512]{2,1,0:T(8,128)(2,1)S(1)} collective-permute-done((bf16[2,512,512]{2,1,0:T(8,128)(2,1)S(1)}, bf16[2,512,512]{2,1,0:T(8,128)(2,1)S(1)}, u32[]{:S(2)}, u32[]{:S(2)}) %collective-permute-start.1) | collective-permute-done | bytes 1048608 | tf_op jit(solution)/shard_map/ppermute | solution.py:59
  62.4 8.0 %collective-permute-start.3 = (bf16[2,512,512]{2,1,0:T(8,128)(2,1)S(1)}, bf16[2,512,512]{2,1,0:T(8,128)(2,1)S(1)}, u32[]{:S(2)}, u32[]{:S(2)}) collective-permute-start(bf16[2,512,512]{2,1,0:T(8,128)(2,1)S(1)} %collective-permute-done.1), channel_id=1, source_target_pairs={{0,2},{2,4},{4,6},{6,8},{8,10},{10,12},{12,14},{14,16},{16,18},{18... | collective-permute-start | bytes 3145736 | tf_op jit(solution)/shard_map/ppermute | solution.py:59
  70.5 8.9 %collective-permute-done.3 = bf16[2,512,512]{2,1,0:T(8,128)(2,1)S(1)} collective-permute-done((bf16[2,512,512]{2,1,0:T(8,128)(2,1)S(1)}, bf16[2,512,512]{2,1,0:T(8,128)(2,1)S(1)}, u32[]{:S(2)}, u32[]{:S(2)}) %collective-permute-start.3) | collective-permute-done | bytes 1048608 | tf_op jit(solution)/shard_map/ppermute | solution.py:59
  79.4 15.8 %collective-permute-start.5 = (bf16[2,512,512]{2,1,0:T(8,128)(2,1)S(1)}, bf16[2,512,512]{2,1,0:T(8,128)(2,1)S(1)}, u32[]{:S(2)}, u32[]{:S(2)}) collective-permute-start(bf16[2,512,512]{2,1,0:T(8,128)(2,1)S(1)} %collective-permute-done.3), channel_id=1, source_target_pairs={{0,2},{2,4},{4,6},{6,8},{8,10},{10,12},{12,14},{14,16},{16,18},{18... | collective-permute-start | bytes 3145736 | tf_op jit(solution)/shard_map/ppermute | solution.py:59
  95.2 3.5 collective-permute-done.5
  99.8 21.1 %collective-permute-start.7 = (bf16[2,512,512]{2,1,0:T(8,128)(2,1)S(1)}, bf16[2,512,512]{2,1,0:T(8,128)(2,1)}, u32[]{:S(2)}, u32[]{:S(2)}) collective-permute-start(bf16[2,512,512]{2,1,0:T(8,128)(2,1)S(1)} %collective-permute-done.5), channel_id=1, source_target_pairs={{0,2},{2,4},{4,6},{6,8},{8,10},{10,12},{12,14},{14,16},{16,18},{18... | collective-permute-start | bytes 3145736 | tf_op jit(solution)/shard_map/ppermute | solution.py:59
  120.9 2.4 collective-permute-done.7
  123.4 22.5 %collective-permute-start.9 = (bf16[2,512,512]{2,1,0:T(8,128)(2,1)}, bf16[2,512,512]{2,1,0:T(8,128)(2,1)}, u32[]{:S(2)}, u32[]{:S(2)}) collective-permute-start(bf16[2,512,512]{2,1,0:T(8,128)(2,1)} %collective-permute-done.7), channel_id=1, source_target_pairs={{0,2},{2,4},{4,6},{6,8},{8,10},{10,12},{12,14},{14,16},{16,18},{18... | collective-permute-start | bytes 3145736 | tf_op jit(solution)/shard_map/ppermute | solution.py:59
  145.8 3.0 reshape.37
  151.1 1.8 convolution_add_fusion.8
  153.3 18.4 %collective-permute-start.11 = (bf16[2,512,512]{2,1,0:T(8,128)(2,1)}, bf16[2,512,512]{2,1,0:T(8,128)(2,1)S(1)}, u32[]{:S(2)}, u32[]{:S(2)}) collective-permute-start(bf16[2,512,512]{2,1,0:T(8,128)(2,1)} %collective-permute-done.9), channel_id=1, source_target_pairs={{0,2},{2,4},{4,6},{6,8},{8,10},{10,12},{12,14},{14,16},{16,18},{18... | collective-permute-start | bytes 3145736 | tf_op jit(solution)/shard_map/ppermute | solution.py:59
  174.6 21.8 %collective-permute-start.13 = (bf16[2,512,512]{2,1,0:T(8,128)(2,1)S(1)}, bf16[2,512,512]{2,1,0:T(8,128)(2,1)S(1)}, u32[]{:S(2)}, u32[]{:S(2)}) collective-permute-start(bf16[2,512,512]{2,1,0:T(8,128)(2,1)S(1)} %collective-permute-done.11), channel_id=1, source_target_pairs={{0,2},{2,4},{4,6},{6,8},{8,10},{10,12},{12,14},{14,16},{16,18},{18... | collective-permute-start | bytes 3145736 | tf_op jit(solution)/shard_map/ppermute | solution.py:59
  201.7 20.0 %collective-permute-start.14 = (bf16[2,512,512]{2,1,0:T(8,128)(2,1)S(1)}, bf16[2,512,512]{2,1,0:T(8,128)(2,1)S(1)}, u32[]{:S(2)}, u32[]{:S(2)}) collective-permute-start(bf16[2,512,512]{2,1,0:T(8,128)(2,1)S(1)} %collective-permute-done.13), channel_id=1, source_target_pairs={{0,2},{2,4},{4,6},{6,8},{8,10},{10,12},{12,14},{14,16},{16,18},{18... | collective-permute-start | bytes 3145736 | tf_op jit(solution)/shard_map/ppermute | solution.py:59
  226.8 1.7 fusion.43
  229.6 1.9 exponential_reduce_fusion
  231.6 4.9 %all-reduce.1 = (f32[192]{0:T(256)S(1)}, f32[192]{0:T(256)S(1)}) all-reduce(f32[192]{0:T(256)S(1)} %get-tuple-element.7, f32[192]{0:T(256)S(1)} %get-tuple-element.6), channel_id=1, replica_groups=mesh['task'=16,'tensor'=2] {'tensor'}, use_global_device_ids=true, to_apply=%region_6.7 | all-reduce | flops 384 | bytes 3072 | tf_op jit(solution)/shard_map/psum | solution.py:97
  237.1 3.6 fusion.1
  240.7 1.9 fusion.36
  245.6 1.7 pad_maximum_fusion
  247.4 2.0 copy.74
  249.4 18.5 %all-to-all-start = ((bf16[192,16,512]{2,0,1:T(8,128)(2,1)}), bf16[192,16,512]{2,0,1:T(8,128)(2,1)S(1)}, u32[]{:S(2)}, u32[]{:S(2)}) async-start(bf16[192,16,512]{2,0,1:T(8,128)(2,1)} %bitcast.132), calls=%async_computation | async-start | bytes 6291456 | tf_op jit(solution)/shard_map/all_to_all | solution.py:117
  267.9 2.7 copy.38
  271.2 92.3 %all-to-all-done = bf16[192,16,512]{2,0,1:T(8,128)(2,1)S(1)} async-done(((bf16[192,16,512]{2,0,1:T(8,128)(2,1)}), bf16[192,16,512]{2,0,1:T(8,128)(2,1)S(1)}, u32[]{:S(2)}, u32[]{:S(2)}) %all-to-all-start) | async-done | bytes 3145760 | tf_op jit(solution)/shard_map/all_to_all | solution.py:117
  363.5 3.1 all-gather.2.cloned.1.call-done
  366.6 7.6 %convolution_bitcast_fusion = f32[2,512,512]{1,2,0:T(8,128)} fusion(bf16[2,3072,512]{2,1,0:T(8,128)(2,1)} %all-gather.2.cloned.1.call-done, bf16[3072,512,1]{1,0,2:T(8,128)(2,1)S(1)} %bitcast.134), kind=kOutput, calls=%fused_computation.17 | convolution fusion | flops 3221225472 | bytes 11534336 | tf_op jit(solution)/shard_map/tr,mtc->mrc/dot_general | solution.py:118
  374.2 1.9 copy.44
  376.1 9.3 %multiply_reduce_fusion = f32[8,2]{1,0:T(8,128)S(1)} fusion(f32[8,2,512,512]{3,2,1,0:T(8,128)} %mul.127, bf16[8,2,512,512]{3,2,1,0:T(8,128)(2,1)} %param.8, f32[2,512,512]{2,1,0:T(8,128)S(1)} %copy.44), kind=kLoop, calls=%fused_computation.1 | loop fusion | flops 16777200 | bytes 27263040 | tf_op jit(solution)/shard_map/reduce_sum | solution.py:124
  386.9 49.4 %all-reduce = (f32[]{:T(128)}, f32[8,2]{1,0:T(8,128)S(1)}) all-reduce(f32[]{:T(128)S(6)} %div.37, f32[8,2]{1,0:T(8,128)S(1)} %multiply_reduce_fusion), channel_id=1, replica_groups=mesh['task'=16,'tensor'=2] {'task','tensor'}, use_global_device_ids=true, to_apply=%region_8.9 | all-reduce | flops 17 | bytes 136 | tf_op jit(solution)/shard_map/psum | solution.py:125
  (92 shorter events, 26.1 us)
Async XLA Ops:
  7.2 359.4 %all-gather.2.cloned.1.call-start = ((), (), s32[]{:S(2)}) async-start(), calls=%async_computation.1 | async-start | bytes 6684672 | tf_op jit(solution)/shard_map/all_gather | solution.py:121
  14.2 19.9 %copy-start.17 = (f32[8,2]{0,1:T(2,128)S(1)}, f32[8,2]{0,1:T(2,128)}, u32[]{:S(2)}) copy-start(f32[8,2]{0,1:T(2,128)} %param.11) | copy-start | bytes 196
  34.2 9.7 %copy-start.11 = (bf16[2,512,512]{2,1,0:T(8,128)(2,1)S(1)}, bf16[2,512,512]{2,1,0:T(8,128)(2,1)}, u32[]{:S(2)}) copy-start(bf16[2,512,512]{2,1,0:T(8,128)(2,1)} %param.9) | copy-start | bytes 3145732
  43.9 105.6 %copy-start = (bf16[192,8192]{1,0:T(8,128)(2,1)S(1)}, bf16[192,8192]{1,0:T(8,128)(2,1)}, u32[]{:S(2)}) copy-start(bf16[192,8192]{1,0:T(8,128)(2,1)} %param.6) | copy-start | bytes 9437188
  44.3 18.1 %collective-permute-start.1 = (bf16[2,512,512]{2,1,0:T(8,128)(2,1)S(1)}, bf16[2,512,512]{2,1,0:T(8,128)(2,1)S(1)}, u32[]{:S(2)}, u32[]{:S(2)}) collective-permute-start(bf16[2,512,512]{2,1,0:T(8,128)(2,1)S(1)} %add_convert_fusion), channel_id=1, source_target_pairs={{0,2},{2,4},{4,6},{6,8},{8,10},{10,12},{12,14},{14,16},{16,18},{18... | collective-permute-start | bytes 3145736 | tf_op jit(solution)/shard_map/ppermute | solution.py:59
  45.3 25.1 %collective-permute-start = (bf16[2,512,512]{2,1,0:T(8,128)(2,1)S(1)}, bf16[2,512,512]{2,1,0:T(8,128)(2,1)S(1)}, u32[]{:S(2)}, u32[]{:S(2)}) collective-permute-start(bf16[2,512,512]{2,1,0:T(8,128)(2,1)S(1)} %add_convert_fusion), channel_id=1, source_target_pairs={{0,30},{2,0},{4,2},{6,4},{8,6},{10,8},{12,10},{14,12},{16,14},{18,... | collective-permute-start | bytes 3145736 | tf_op jit(solution)/shard_map/ppermute | solution.py:61
  62.4 8.0 %copy-start.4 = (bf16[2,512,512]{2,1,0:T(8,128)(2,1)}, bf16[2,512,512]{2,1,0:T(8,128)(2,1)S(1)}, u32[]{:S(2)}) copy-start(bf16[2,512,512]{2,1,0:T(8,128)(2,1)S(1)} %collective-permute-done.1) | copy-start | bytes 3145732
  62.4 17.0 %collective-permute-start.3 = (bf16[2,512,512]{2,1,0:T(8,128)(2,1)S(1)}, bf16[2,512,512]{2,1,0:T(8,128)(2,1)S(1)}, u32[]{:S(2)}, u32[]{:S(2)}) collective-permute-start(bf16[2,512,512]{2,1,0:T(8,128)(2,1)S(1)} %collective-permute-done.1), channel_id=1, source_target_pairs={{0,2},{2,4},{4,6},{6,8},{8,10},{10,12},{12,14},{14,16},{16,18},{18... | collective-permute-start | bytes 3145736 | tf_op jit(solution)/shard_map/ppermute | solution.py:59
  70.4 9.0 %copy-start.6 = (bf16[2,512,512]{2,1,0:T(8,128)(2,1)}, bf16[2,512,512]{2,1,0:T(8,128)(2,1)S(1)}, u32[]{:S(2)}) copy-start(bf16[2,512,512]{2,1,0:T(8,128)(2,1)S(1)} %collective-permute-done) | copy-start | bytes 3145732
  70.4 24.7 %collective-permute-start.2 = (bf16[2,512,512]{2,1,0:T(8,128)(2,1)S(1)}, bf16[2,512,512]{2,1,0:T(8,128)(2,1)S(1)}, u32[]{:S(2)}, u32[]{:S(2)}) collective-permute-start(bf16[2,512,512]{2,1,0:T(8,128)(2,1)S(1)} %collective-permute-done), channel_id=1, source_target_pairs={{0,30},{2,0},{4,2},{6,4},{8,6},{10,8},{12,10},{14,12},{16,14},{18,... | collective-permute-start | bytes 3145736 | tf_op jit(solution)/shard_map/ppermute | solution.py:61
  79.4 15.8 %copy-start.7 = (bf16[2,512,512]{2,1,0:T(8,128)(2,1)}, bf16[2,512,512]{2,1,0:T(8,128)(2,1)S(1)}, u32[]{:S(2)}) copy-start(bf16[2,512,512]{2,1,0:T(8,128)(2,1)S(1)} %collective-permute-done.3) | copy-start | bytes 3145732
  79.4 19.4 %collective-permute-start.5 = (bf16[2,512,512]{2,1,0:T(8,128)(2,1)S(1)}, bf16[2,512,512]{2,1,0:T(8,128)(2,1)S(1)}, u32[]{:S(2)}, u32[]{:S(2)}) collective-permute-start(bf16[2,512,512]{2,1,0:T(8,128)(2,1)S(1)} %collective-permute-done.3), channel_id=1, source_target_pairs={{0,2},{2,4},{4,6},{6,8},{8,10},{10,12},{12,14},{14,16},{16,18},{18... | collective-permute-start | bytes 3145736 | tf_op jit(solution)/shard_map/ppermute | solution.py:59
  95.1 28.2 %copy-start.12 = (bf16[2,512,512]{2,1,0:T(8,128)(2,1)}, bf16[2,512,512]{2,1,0:T(8,128)(2,1)S(1)}, u32[]{:S(2)}) copy-start(bf16[2,512,512]{2,1,0:T(8,128)(2,1)S(1)} %collective-permute-done.2) | copy-start | bytes 3145732
  95.2 25.8 %collective-permute-start.4 = (bf16[2,512,512]{2,1,0:T(8,128)(2,1)S(1)}, bf16[2,512,512]{2,1,0:T(8,128)(2,1)}, u32[]{:S(2)}, u32[]{:S(2)}) collective-permute-start(bf16[2,512,512]{2,1,0:T(8,128)(2,1)S(1)} %collective-permute-done.2), channel_id=1, source_target_pairs={{0,30},{2,0},{4,2},{6,4},{8,6},{10,8},{12,10},{14,12},{16,14},{18,... | collective-permute-start | bytes 3145736 | tf_op jit(solution)/shard_map/ppermute | solution.py:61
  99.8 23.6 %collective-permute-start.7 = (bf16[2,512,512]{2,1,0:T(8,128)(2,1)S(1)}, bf16[2,512,512]{2,1,0:T(8,128)(2,1)}, u32[]{:S(2)}, u32[]{:S(2)}) collective-permute-start(bf16[2,512,512]{2,1,0:T(8,128)(2,1)S(1)} %collective-permute-done.5), channel_id=1, source_target_pairs={{0,2},{2,4},{4,6},{6,8},{8,10},{10,12},{12,14},{14,16},{16,18},{18... | collective-permute-start | bytes 3145736 | tf_op jit(solution)/shard_map/ppermute | solution.py:59
  120.9 31.9 %collective-permute-start.6 = (bf16[2,512,512]{2,1,0:T(8,128)(2,1)}, bf16[2,512,512]{2,1,0:T(8,128)(2,1)}, u32[]{:S(2)}, u32[]{:S(2)}) collective-permute-start(bf16[2,512,512]{2,1,0:T(8,128)(2,1)} %collective-permute-done.4), channel_id=1, source_target_pairs={{0,30},{2,0},{4,2},{6,4},{8,6},{10,8},{12,10},{14,12},{16,14},{18,... | collective-permute-start | bytes 3145736 | tf_op jit(solution)/shard_map/ppermute | solution.py:61
  123.4 30.0 %collective-permute-start.9 = (bf16[2,512,512]{2,1,0:T(8,128)(2,1)}, bf16[2,512,512]{2,1,0:T(8,128)(2,1)}, u32[]{:S(2)}, u32[]{:S(2)}) collective-permute-start(bf16[2,512,512]{2,1,0:T(8,128)(2,1)} %collective-permute-done.7), channel_id=1, source_target_pairs={{0,2},{2,4},{4,6},{6,8},{8,10},{10,12},{12,14},{14,16},{16,18},{18... | collective-permute-start | bytes 3145736 | tf_op jit(solution)/shard_map/ppermute | solution.py:59
  148.8 4.1 copy-start.5
  151.1 20.7 %copy-start.8 = (bf16[2,512,512]{2,1,0:T(8,128)(2,1)S(1)}, bf16[2,512,512]{2,1,0:T(8,128)(2,1)}, u32[]{:S(2)}) copy-start(bf16[2,512,512]{2,1,0:T(8,128)(2,1)} %copy-done.7) | copy-start | bytes 3145732
  151.1 21.0 %copy-start.13 = (bf16[2,512,512]{2,1,0:T(8,128)(2,1)S(1)}, bf16[2,512,512]{2,1,0:T(8,128)(2,1)}, u32[]{:S(2)}) copy-start(bf16[2,512,512]{2,1,0:T(8,128)(2,1)} %copy-done.12) | copy-start | bytes 3145732
  152.9 20.0 %collective-permute-start.8 = (bf16[2,512,512]{2,1,0:T(8,128)(2,1)}, bf16[2,512,512]{2,1,0:T(8,128)(2,1)S(1)}, u32[]{:S(2)}, u32[]{:S(2)}) collective-permute-start(bf16[2,512,512]{2,1,0:T(8,128)(2,1)} %collective-permute-done.6), channel_id=1, source_target_pairs={{0,30},{2,0},{4,2},{6,4},{8,6},{10,8},{12,10},{14,12},{16,14},{18,... | collective-permute-start | bytes 3145736 | tf_op jit(solution)/shard_map/ppermute | solution.py:61
  153.3 19.2 %copy-start.10 = (bf16[2,512,512]{2,1,0:T(8,128)(2,1)S(1)}, bf16[2,512,512]{2,1,0:T(8,128)(2,1)}, u32[]{:S(2)}) copy-start(bf16[2,512,512]{2,1,0:T(8,128)(2,1)} %copy-done.9) | copy-start | bytes 3145732
  153.3 21.2 %collective-permute-start.11 = (bf16[2,512,512]{2,1,0:T(8,128)(2,1)}, bf16[2,512,512]{2,1,0:T(8,128)(2,1)S(1)}, u32[]{:S(2)}, u32[]{:S(2)}) collective-permute-start(bf16[2,512,512]{2,1,0:T(8,128)(2,1)} %collective-permute-done.9), channel_id=1, source_target_pairs={{0,2},{2,4},{4,6},{6,8},{8,10},{10,12},{12,14},{14,16},{16,18},{18... | collective-permute-start | bytes 3145736 | tf_op jit(solution)/shard_map/ppermute | solution.py:59
  172.9 28.3 %collective-permute-start.10 = (bf16[2,512,512]{2,1,0:T(8,128)(2,1)S(1)}, bf16[2,512,512]{2,1,0:T(8,128)(2,1)S(1)}, u32[]{:S(2)}, u32[]{:S(2)}) collective-permute-start(bf16[2,512,512]{2,1,0:T(8,128)(2,1)S(1)} %collective-permute-done.8), channel_id=1, source_target_pairs={{0,30},{2,0},{4,2},{6,4},{8,6},{10,8},{12,10},{14,12},{16,14},{18,... | collective-permute-start | bytes 3145736 | tf_op jit(solution)/shard_map/ppermute | solution.py:61
  174.6 27.1 %collective-permute-start.13 = (bf16[2,512,512]{2,1,0:T(8,128)(2,1)S(1)}, bf16[2,512,512]{2,1,0:T(8,128)(2,1)S(1)}, u32[]{:S(2)}, u32[]{:S(2)}) collective-permute-start(bf16[2,512,512]{2,1,0:T(8,128)(2,1)S(1)} %collective-permute-done.11), channel_id=1, source_target_pairs={{0,2},{2,4},{4,6},{6,8},{8,10},{10,12},{12,14},{14,16},{16,18},{18... | collective-permute-start | bytes 3145736 | tf_op jit(solution)/shard_map/ppermute | solution.py:59
  201.2 21.7 %collective-permute-start.12 = (bf16[2,512,512]{2,1,0:T(8,128)(2,1)S(1)}, bf16[2,512,512]{2,1,0:T(8,128)(2,1)S(1)}, u32[]{:S(2)}, u32[]{:S(2)}) collective-permute-start(bf16[2,512,512]{2,1,0:T(8,128)(2,1)S(1)} %collective-permute-done.10), channel_id=1, source_target_pairs={{0,30},{2,0},{4,2},{6,4},{8,6},{10,8},{12,10},{14,12},{16,14},{18,... | collective-permute-start | bytes 3145736 | tf_op jit(solution)/shard_map/ppermute | solution.py:61
  201.7 22.3 %collective-permute-start.14 = (bf16[2,512,512]{2,1,0:T(8,128)(2,1)S(1)}, bf16[2,512,512]{2,1,0:T(8,128)(2,1)S(1)}, u32[]{:S(2)}, u32[]{:S(2)}) collective-permute-start(bf16[2,512,512]{2,1,0:T(8,128)(2,1)S(1)} %collective-permute-done.13), channel_id=1, source_target_pairs={{0,2},{2,4},{4,6},{6,8},{8,10},{10,12},{12,14},{14,16},{16,18},{18... | collective-permute-start | bytes 3145736 | tf_op jit(solution)/shard_map/ppermute | solution.py:59
  229.6 1.9 copy-start.18
  237.1 3.6 copy-start.14
  237.1 3.6 copy-start.19
  249.4 114.1 %all-to-all-start = ((bf16[192,16,512]{2,0,1:T(8,128)(2,1)}), bf16[192,16,512]{2,0,1:T(8,128)(2,1)S(1)}, u32[]{:S(2)}, u32[]{:S(2)}) async-start(bf16[192,16,512]{2,0,1:T(8,128)(2,1)} %bitcast.132), calls=%async_computation | async-start | bytes 6291456 | tf_op jit(solution)/shard_map/all_to_all | solution.py:117
  376.1 9.3 %copy-start.2 = (bf16[192,4,4,128]{3,2,1,0:T(4,128)(2,1)S(1)}, bf16[192,4,4,128]{3,2,1,0:T(4,128)(2,1)}, u32[]{:S(2)}) copy-start(bf16[192,4,4,128]{3,2,1,0:T(4,128)(2,1)} %copy.38) | copy-start | bytes 2359300
  (5 other events, 6.8 us)
Sparse Core Ops, SparseCore 0:
  247.5 119.0 all-gather.1
